TPU v7x, 512 devices: a whole 4x8x8 slice. The times are simulated.
512 devices in a mesh: pb: 32 (over x, z), ao: 16 (over y, core).
Axes of the slice: x: 4, y: 8, z: 8, core: 2. Of those that a mesh axis runs over, the one named last changes fastest.
Arguments:
- queries: bfloat16 [32768, 128], P('pb'), may hold values from -4 to 4
- centres: bfloat16 [32768, 128], P(('pb', 'ao')), may hold values from -4 to 4
- coefs: bfloat16 [32768, 4096], P('pb', 'ao'), may hold values from -3 to 3
- pattern: int32 [32, 5], replicated, may hold values from 0 to 1, as said below
Outputs:
- scores: bfloat16 [32768, 4096], P('pb', 'ao')
Inputs may be any that keep to these rules, and one draw needn't show every extreme that they name: pattern[i, j] tells whether query block i lists centre block i + j - 2; it is 0 where that block lies outside 0 to 31, and 1 for j = 2.
All inputs are finite; a program needn't handle non-finite values.
Results may differ from a plain program's by a relative error of at most 0.0049.
Values may be sent and summed in bfloat16 or wider, within the bound.
A program may use at most 64 MiB of HBM per device.

v0:
```python
import math
import jax
import jax.numpy as jnp
from jax import lax
from jax.sharding import PartitionSpec as P

RADIUS_FACTOR = 1.3


def shifted(block, axis, distance):
    devices = range(lax.axis_size(axis))
    route = [(i - distance, i) for i in devices if i - distance in devices]
    return lax.ppermute(block, axis, route)


def query_norms(query_rows):
    query_wide = query_rows.astype(jnp.float32)
    return jnp.sum(query_wide * query_wide, axis=1)[:, None]


def wendland_block(query_rows, query_norm, centre_rows):
    centre_wide = centre_rows.astype(jnp.float32)
    centre_norm = jnp.sum(centre_wide * centre_wide, axis=1)[None, :]
    cross = jnp.dot(query_rows, centre_rows.T, preferred_element_type=jnp.float32)
    dist = jnp.sqrt(query_norm + centre_norm - 2.0 * cross)
    scaled = dist / (RADIUS_FACTOR * math.sqrt(query_rows.shape[1]))
    inner = jnp.maximum(1.0 - scaled, 0.0)
    return inner * inner * inner * inner * (4.0 * scaled + 1.0)


def contribute(query_rows, query_norm, centre_rows, coef_rows, weight):
    kern = (
        wendland_block(query_rows, query_norm, centre_rows) * weight.astype(jnp.float32)
    ).astype(jnp.bfloat16)
    return jnp.dot(kern, coef_rows, preferred_element_type=jnp.float32)


def per_device(queries, centres, coefs, pattern):
    band_width = pattern.shape[1]
    half_band = band_width // 2
    my_block = lax.axis_index("pb")
    my_pattern = lax.dynamic_index_in_dim(pattern, my_block, 0, keepdims=False)
    panel_coords = lax.all_gather(centres, "ao", axis=0, tiled=True)
    my_norm = query_norms(queries)
    offsets = [shift_by for shift_by in range(-half_band, half_band + 1) if shift_by != 0]
    accumulated = contribute(queries, my_norm, panel_coords, coefs, my_pattern[half_band])
    for shift_by in offsets:
        far_coords, far_coefs = shifted((panel_coords, coefs), "pb", -shift_by)
        accumulated = accumulated + contribute(
            queries, my_norm, far_coords, far_coefs, my_pattern[half_band + shift_by]
        )
    return accumulated.astype(jnp.bfloat16)


def solution(mesh):
    in_specs = (P("pb", None), P(("pb", "ao"), None), P("pb", "ao"), P())
    out_specs = P("pb", "ao")
    return jax.shard_map(
        per_device, mesh=mesh, in_specs=in_specs, out_specs=out_specs, check_vma=False
    )
```

profile of v0, /device:TPU:2, one launch (start us, length us, event | category | flops | bytes accessed | tf_op | source)
XLA Modules:
  0.0 104.8 jit_solution(7479997999850689913)
XLA Ops:
  0.0 18.7 %all_gather.3 = bf16[1024,128]{1,0:T(8,128)(2,1)S(1)} all-gather(bf16[64,128]{1,0:T(8,128)(2,1)} %param.5), channel_id=1, replica_groups=mesh['pb'=32,'ao'=16] {'ao'}, dimensions={0}, use_global_device_ids=true | all-gather | bytes 278528 | tf_op jit(solution)/shard_map/all_gather | solution.py:43
  18.7 10.9 %collective-permute-start.6 = (bf16[1024,128]{1,0:T(8,128)(2,1)S(1)}, bf16[1024,128]{1,0:T(8,128)(2,1)S(1)}, u32[]{:S(2)}, u32[]{:S(2)}) collective-permute-start(bf16[1024,128]{1,0:T(8,128)(2,1)S(1)} %all_gather.3), channel_id=1, source_target_pairs={{32,0},{48,16},{64,32},{80,48},{96,64},{112,80},{128,96},{144,112}... | collective-permute-start | bytes 786440 | tf_op jit(solution)/shard_map/ppermute | solution.py:13
  29.6 2.5 %collective-permute-start.4 = (bf16[1024,128]{1,0:T(8,128)(2,1)S(1)}, bf16[1024,128]{1,0:T(8,128)(2,1)S(1)}, u32[]{:S(2)}, u32[]{:S(2)}) collective-permute-start(bf16[1024,128]{1,0:T(8,128)(2,1)S(1)} %all_gather.3), channel_id=1, source_target_pairs={{16,0},{32,16},{48,32},{64,48},{80,64},{96,80},{112,96},{128,112},... | collective-permute-start | bytes 786440 | tf_op jit(solution)/shard_map/ppermute | solution.py:13
  32.0 3.4 %collective-permute-start.2 = (bf16[1024,128]{1,0:T(8,128)(2,1)S(1)}, bf16[1024,128]{1,0:T(8,128)(2,1)S(1)}, u32[]{:S(2)}, u32[]{:S(2)}) collective-permute-start(bf16[1024,128]{1,0:T(8,128)(2,1)S(1)} %all_gather.3), channel_id=1, source_target_pairs={{0,16},{16,32},{32,48},{48,64},{64,80},{80,96},{96,112},{112,128},... | collective-permute-start | bytes 786440 | tf_op jit(solution)/shard_map/ppermute | solution.py:13
  35.4 2.8 %collective-permute-start = (bf16[1024,128]{1,0:T(8,128)(2,1)S(1)}, bf16[1024,128]{1,0:T(8,128)(2,1)S(1)}, u32[]{:S(2)}, u32[]{:S(2)}) collective-permute-start(bf16[1024,128]{1,0:T(8,128)(2,1)S(1)} %all_gather.3), channel_id=1, source_target_pairs={{0,32},{16,48},{32,64},{48,80},{64,96},{80,112},{96,128},{112,144}... | collective-permute-start | bytes 786440 | tf_op jit(solution)/shard_map/ppermute | solution.py:13
  38.3 2.5 %collective-permute-start.3 = (bf16[1024,256]{1,0:T(8,128)(2,1)}, bf16[1024,256]{1,0:T(8,128)(2,1)S(1)}, u32[]{:S(2)}, u32[]{:S(2)}) collective-permute-start(bf16[1024,256]{1,0:T(8,128)(2,1)} %param.6), channel_id=1, source_target_pairs={{0,16},{16,32},{32,48},{48,64},{64,80},{80,96},{96,112},{112,128},... | collective-permute-start | bytes 1572872 | tf_op jit(solution)/shard_map/ppermute | solution.py:13
  40.7 0.2 multiply_reduce_fusion.4
  41.0 0.6 fusion.50
  42.4 1.2 %multiply_reduce_fusion.5 = f32[1024]{0:T(1024)S(1)} fusion(bf16[1024,128]{1,0:T(8,128)(2,1)} %param.4), kind=kLoop, calls=%fused_computation.35 | loop fusion | flops 392192 | bytes 266240 | tf_op jit(solution)/shard_map/reduce_sum | solution.py:18
  43.5 5.2 %fusion.19 = f32[1024,256]{1,0:T(8,128)} fusion(bf16[1024,256]{1,0:T(8,128)(2,1)} %param.6, bf16[1024,128]{1,0:T(8,128)(2,1)} %param.4, bf16[1024,128]{1,0:T(8,128)(2,1)S(1)} %all_gather.3, f32[]{:T(128)} %bitcast, f32[1024]{0:T(1024)S(1)} %multiply_reduce_fusion.4, f32[1024]{0:T(1024)S(1)} %multiply_reduce_fusion.5), kind=kOutput, calls=%fused_computation.24 | convolution fusion | flops 819986432 | bytes 2105348 | tf_op jit(solution)/shard_map/dot_general | solution.py:35
  51.4 2.5 %collective-permute-start.1 = (bf16[1024,256]{1,0:T(8,128)(2,1)S(1)}, bf16[1024,256]{1,0:T(8,128)(2,1)S(1)}, u32[]{:S(2)}, u32[]{:S(2)}) collective-permute-start(bf16[1024,256]{1,0:T(8,128)(2,1)S(1)} %copy-done.2), channel_id=1, source_target_pairs={{0,32},{16,48},{32,64},{48,80},{64,96},{80,112},{96,128},{112,144}... | collective-permute-start | bytes 1572872 | tf_op jit(solution)/shard_map/ppermute | solution.py:13
  53.9 0.2 multiply_reduce_fusion
  54.1 6.4 %collective-permute-start.7 = (bf16[1024,256]{1,0:T(8,128)(2,1)S(1)}, bf16[1024,256]{1,0:T(8,128)(2,1)}, u32[]{:S(2)}, u32[]{:S(2)}) collective-permute-start(bf16[1024,256]{1,0:T(8,128)(2,1)S(1)} %copy-done.2), channel_id=1, source_target_pairs={{32,0},{48,16},{64,32},{80,48},{96,64},{112,80},{128,96},{144,112}... | collective-permute-start | bytes 1572872 | tf_op jit(solution)/shard_map/ppermute | solution.py:13
  60.5 0.2 multiply_reduce_fusion.1
  60.7 3.6 %collective-permute-start.5 = (bf16[1024,256]{1,0:T(8,128)(2,1)S(1)}, bf16[1024,256]{1,0:T(8,128)(2,1)}, u32[]{:S(2)}, u32[]{:S(2)}) collective-permute-start(bf16[1024,256]{1,0:T(8,128)(2,1)S(1)} %copy-done.2), channel_id=1, source_target_pairs={{16,0},{32,16},{48,32},{64,48},{80,64},{96,80},{112,96},{128,112},... | collective-permute-start | bytes 1572872 | tf_op jit(solution)/shard_map/ppermute | solution.py:13
  64.3 0.2 multiply_reduce_fusion.2
  64.5 0.2 multiply_reduce_fusion.3
  64.7 13.2 %collective-permute-done.3 = bf16[1024,256]{1,0:T(8,128)(2,1)S(1)} collective-permute-done((bf16[1024,256]{1,0:T(8,128)(2,1)}, bf16[1024,256]{1,0:T(8,128)(2,1)S(1)}, u32[]{:S(2)}, u32[]{:S(2)}) %collective-permute-start.3) | collective-permute-done | bytes 524320 | tf_op jit(solution)/shard_map/ppermute | solution.py:13
  77.9 4.1 %fusion.17 = f32[1024,256]{1,0:T(8,128)} fusion(bf16[1024,256]{1,0:T(8,128)(2,1)S(1)} %collective-permute-done.3, bf16[1024,128]{1,0:T(8,128)(2,1)S(1)} %copy-done.1, bf16[1024,128]{1,0:T(8,128)(2,1)S(1)} %collective-permute-done.2, f32[]{:T(128)} %bitcast.2, f32[1024]{0:T(1024)S(1)} %multiply_reduce_fusion.2, f32[1024]{0:T(1024)S(1)} %multiply_reduce_fusion.5), kind=kOutput, calls=%fused_computation.22 | convolution fusion | flops 819986432 | bytes 2105348 | tf_op jit(solution)/shard_map/dot_general | solution.py:35
  82.0 1.8 %collective-permute-done.7 = bf16[1024,256]{1,0:T(8,128)(2,1)} collective-permute-done((bf16[1024,256]{1,0:T(8,128)(2,1)S(1)}, bf16[1024,256]{1,0:T(8,128)(2,1)}, u32[]{:S(2)}, u32[]{:S(2)}) %collective-permute-start.7) | collective-permute-done | bytes 524320 | tf_op jit(solution)/shard_map/ppermute | solution.py:13
  83.8 5.1 %fusion.15 = f32[1024,256]{1,0:T(8,128)} fusion(bf16[1024,256]{1,0:T(8,128)(2,1)} %collective-permute-done.7, bf16[1024,128]{1,0:T(8,128)(2,1)S(1)} %copy-done.1, bf16[1024,128]{1,0:T(8,128)(2,1)S(1)} %collective-permute-done.6, f32[]{:T(128)} %bitcast.4, f32[1024]{0:T(1024)S(1)} %multiply_reduce_fusion, f32[1024]{0:T(1024)S(1)} %multiply_reduce_fusion.5), kind=kOutput, calls=%fused_computation.20 | convolution fusion | flops 819986432 | bytes 2105348 | tf_op jit(solution)/shard_map/dot_general | solution.py:35
  88.9 5.2 %collective-permute-done.5 = bf16[1024,256]{1,0:T(8,128)(2,1)} collective-permute-done((bf16[1024,256]{1,0:T(8,128)(2,1)S(1)}, bf16[1024,256]{1,0:T(8,128)(2,1)}, u32[]{:S(2)}, u32[]{:S(2)}) %collective-permute-start.5) | collective-permute-done | bytes 524320 | tf_op jit(solution)/shard_map/ppermute | solution.py:13
  94.1 5.1 %fusion.16 = f32[1024,256]{1,0:T(8,128)} fusion(bf16[1024,256]{1,0:T(8,128)(2,1)} %collective-permute-done.5, bf16[1024,128]{1,0:T(8,128)(2,1)S(1)} %copy-done.1, bf16[1024,128]{1,0:T(8,128)(2,1)S(1)} %collective-permute-done.4, f32[]{:T(128)} %bitcast.3, f32[1024]{0:T(1024)S(1)} %multiply_reduce_fusion.1, f32[1024]{0:T(1024)S(1)} %multiply_reduce_fusion.5), kind=kOutput, calls=%fused_computation.21 | convolution fusion | flops 819986432 | bytes 2105348 | tf_op jit(solution)/shard_map/dot_general | solution.py:35
  99.2 5.6 %fusion.24 = bf16[1024,256]{1,0:T(8,128)(2,1)} fusion(f32[1024,256]{1,0:T(8,128)} %fusion.15, f32[1024,256]{1,0:T(8,128)} %fusion.16, f32[1024,256]{1,0:T(8,128)} %fusion.17, f32[1024,256]{1,0:T(8,128)} %fusion.19, bf16[1024,256]{1,0:T(8,128)(2,1)S(1)} %collective-permute-done.1, bf16[1024,128]{1,0:T(8,128)(2,1)S(1)} %copy-done.1, ...), kind=kOutput, calls=%fused_computation.29 | convolution fusion | flops 821297152 | bytes 5775364 | tf_op jit(solution)/shard_map/dot_general | solution.py:35
  (12 shorter events, 0.1 us)
Async XLA Ops:
  0.0 41.0 %copy-start = (s32[32,5]{0,1:T(8,128)S(1)}, s32[32,5]{0,1:T(8,128)}, u32[]{:S(2)}) copy-start(s32[32,5]{0,1:T(8,128)} %param.7) | copy-start | bytes 1924
  18.7 32.7 %collective-permute-start.6 = (bf16[1024,128]{1,0:T(8,128)(2,1)S(1)}, bf16[1024,128]{1,0:T(8,128)(2,1)S(1)}, u32[]{:S(2)}, u32[]{:S(2)}) collective-permute-start(bf16[1024,128]{1,0:T(8,128)(2,1)S(1)} %all_gather.3), channel_id=1, source_target_pairs={{32,0},{48,16},{64,32},{80,48},{96,64},{112,80},{128,96},{144,112}... | collective-permute-start | bytes 786440 | tf_op jit(solution)/shard_map/ppermute | solution.py:13
  29.6 24.6 %collective-permute-start.4 = (bf16[1024,128]{1,0:T(8,128)(2,1)S(1)}, bf16[1024,128]{1,0:T(8,128)(2,1)S(1)}, u32[]{:S(2)}, u32[]{:S(2)}) collective-permute-start(bf16[1024,128]{1,0:T(8,128)(2,1)S(1)} %all_gather.3), channel_id=1, source_target_pairs={{16,0},{32,16},{48,32},{64,48},{80,64},{96,80},{112,96},{128,112},... | collective-permute-start | bytes 786440 | tf_op jit(solution)/shard_map/ppermute | solution.py:13
  32.0 28.7 %collective-permute-start.2 = (bf16[1024,128]{1,0:T(8,128)(2,1)S(1)}, bf16[1024,128]{1,0:T(8,128)(2,1)S(1)}, u32[]{:S(2)}, u32[]{:S(2)}) collective-permute-start(bf16[1024,128]{1,0:T(8,128)(2,1)S(1)} %all_gather.3), channel_id=1, source_target_pairs={{0,16},{16,32},{32,48},{48,64},{64,80},{80,96},{96,112},{112,128},... | collective-permute-start | bytes 786440 | tf_op jit(solution)/shard_map/ppermute | solution.py:13
  35.4 29.1 %collective-permute-start = (bf16[1024,128]{1,0:T(8,128)(2,1)S(1)}, bf16[1024,128]{1,0:T(8,128)(2,1)S(1)}, u32[]{:S(2)}, u32[]{:S(2)}) collective-permute-start(bf16[1024,128]{1,0:T(8,128)(2,1)S(1)} %all_gather.3), channel_id=1, source_target_pairs={{0,32},{16,48},{32,64},{48,80},{64,96},{80,112},{96,128},{112,144}... | collective-permute-start | bytes 786440 | tf_op jit(solution)/shard_map/ppermute | solution.py:13
  38.3 39.7 %collective-permute-start.3 = (bf16[1024,256]{1,0:T(8,128)(2,1)}, bf16[1024,256]{1,0:T(8,128)(2,1)S(1)}, u32[]{:S(2)}, u32[]{:S(2)}) collective-permute-start(bf16[1024,256]{1,0:T(8,128)(2,1)} %param.6), channel_id=1, source_target_pairs={{0,16},{16,32},{32,48},{48,64},{64,80},{80,96},{96,112},{112,128},... | collective-permute-start | bytes 1572872 | tf_op jit(solution)/shard_map/ppermute | solution.py:13
  43.5 7.9 %copy-start.2 = (bf16[1024,256]{1,0:T(8,128)(2,1)S(1)}, bf16[1024,256]{1,0:T(8,128)(2,1)}, u32[]{:S(2)}) copy-start(bf16[1024,256]{1,0:T(8,128)(2,1)} %param.6) | copy-start | bytes 1572868
  48.8 29.2 %copy-start.1 = (bf16[1024,128]{1,0:T(8,128)(2,1)S(1)}, bf16[1024,128]{1,0:T(8,128)(2,1)}, u32[]{:S(2)}) copy-start(bf16[1024,128]{1,0:T(8,128)(2,1)} %param.4) | copy-start | bytes 786436
  51.4 47.8 %collective-permute-start.1 = (bf16[1024,256]{1,0:T(8,128)(2,1)S(1)}, bf16[1024,256]{1,0:T(8,128)(2,1)S(1)}, u32[]{:S(2)}, u32[]{:S(2)}) collective-permute-start(bf16[1024,256]{1,0:T(8,128)(2,1)S(1)} %copy-done.2), channel_id=1, source_target_pairs={{0,32},{16,48},{32,64},{48,80},{64,96},{80,112},{96,128},{112,144}... | collective-permute-start | bytes 1572872 | tf_op jit(solution)/shard_map/ppermute | solution.py:13
  54.1 29.7 %collective-permute-start.7 = (bf16[1024,256]{1,0:T(8,128)(2,1)S(1)}, bf16[1024,256]{1,0:T(8,128)(2,1)}, u32[]{:S(2)}, u32[]{:S(2)}) collective-permute-start(bf16[1024,256]{1,0:T(8,128)(2,1)S(1)} %copy-done.2), channel_id=1, source_target_pairs={{32,0},{48,16},{64,32},{80,48},{96,64},{112,80},{128,96},{144,112}... | collective-permute-start | bytes 1572872 | tf_op jit(solution)/shard_map/ppermute | solution.py:13
  60.7 33.4 %collective-permute-start.5 = (bf16[1024,256]{1,0:T(8,128)(2,1)S(1)}, bf16[1024,256]{1,0:T(8,128)(2,1)}, u32[]{:S(2)}, u32[]{:S(2)}) collective-permute-start(bf16[1024,256]{1,0:T(8,128)(2,1)S(1)} %copy-done.2), channel_id=1, source_target_pairs={{16,0},{32,16},{48,32},{64,48},{80,64},{96,80},{112,96},{128,112},... | collective-permute-start | bytes 1572872 | tf_op jit(solution)/shard_map/ppermute | solution.py:13
where the time goes:
time: 105 us
  starting transfers between devices  34.4 us (33%)
  matrix products  25.1 us (24%)
  waiting for transfers between devices  20.2 us (19%)
  blocking collectives  18.7 us (18%)
  between operations  3.51 us (3%)
  other arithmetic  2.2 us (2%)
    ppermute x8, starting transfers between devices, shifted(): return lax.ppermute(block, axis, route)  34.4 us
    dot_general x5, matrix products, contribute(): return jnp.dot(kern, coef_rows, preferred_element_type=jnp.float32)  25.1 us
    ppermute x8, waiting for transfers between devices, shifted(): return lax.ppermute(block, axis, route)  20.2 us
    all_gather x1, blocking collectives, per_device(): panel_coords = lax.all_gather(centres, 'ao', axis=0, tiled=True)  18.7 us
  transfers between devices with their start and end apart: 8, of which 3 were waited for; matrix products, arithmetic and copies ran while one was open for 21% of the time, Pallas kernels for 0%

commit v1 on v0

--- a/solution.py
+++ b/solution.py
@@ -5,6 +5,17 @@
 from jax.sharding import PartitionSpec as P
 
 RADIUS_FACTOR = 1.3
+
+
+def replace_panel_for(my_tile, ax_name="ao"):
+    shaped = lax.all_to_all(
+        jnp.stack([my_tile for _ in range(lax.axis_size(ax_name))], 0),
+        concat_axis=0,
+        axis_name=ax_name,
+        split_axis=0,
+    )
+    long_array = jnp.concatenate(shaped, 0)
+    return long_array
 
 
 def shifted(block, axis, distance):
@@ -40,7 +51,7 @@
     half_band = band_width // 2
     my_block = lax.axis_index("pb")
     my_pattern = lax.dynamic_index_in_dim(pattern, my_block, 0, keepdims=False)
-    panel_coords = lax.all_gather(centres, "ao", axis=0, tiled=True)
+    panel_coords = replace_panel_for(centres)
     my_norm = query_norms(queries)
     offsets = [shift_by for shift_by in range(-half_band, half_band + 1) if shift_by != 0]
     accumulated = contribute(queries, my_norm, panel_coords, coefs, my_pattern[half_band])

time: 105 us -> 101 us (0.962)
  blocking collectives: 18.7 us -> 0 us
  starting transfers between devices: 34.4 us -> 43.3 us
  waiting for transfers between devices: 20.2 us -> 25.3 us
  local copies, waits for them, and re-layouts: 0.7 us -> 2.31 us
  matrix products: 25.1 us -> 24 us
    all_gather x1 -> x0, blocking collectives: 18.7 us -> none  [per_device(): panel_coords = lax.all_gather(centres, 'ao', axis=0, tiled=True)]
    all_to_all x0 -> x1, starting transfers between devices: none -> 7.21 us  [replace_panel_for(): lax.all_to_all(jnp.stack([my_tile for _ in range(lax.axis_size(ax_name))]...]
    ppermute x8, waiting for transfers between devices: 20.2 us -> 25.2 us  [shifted(): return lax.ppermute(block, axis, route)]
    ppermute x8, starting transfers between devices: 34.4 us -> 36.1 us  [shifted(): return lax.ppermute(block, axis, route)]
    another operation x0 -> x1, local copies, waits for them, and re-layouts: none -> 1.55 us  [replace_panel_for(): jnp.stack([my_tile for _ in range(lax.axis_size(ax_name))], 0)]
    dot_general x5, matrix products: 25.1 us -> 24 us  [contribute(): return jnp.dot(kern, coef_rows, preferred_element_type=jnp.float32)]
  transfers between devices with their start and end apart: 8 -> 9, of which waited for: 3 -> 5; matrix products, arithmetic and copies ran while one was open for 21% -> 21% of each run, Pallas kernels for 0% -> 0%
where the time goes in v1:
time: 101 us; the launch traced here: 100 us
  starting transfers between devices  43.3 us (43%)
  waiting for transfers between devices  25.3 us (25%)
  matrix products  24 us (24%)
  between operations  3.33 us (3%)
  local copies, waits for them, and re-layouts  2.31 us (2%)
  other arithmetic  2.2 us (2%)
    ppermute x8, starting transfers between devices, shifted(): return lax.ppermute(block, axis, route)  36.1 us
    ppermute x8, waiting for transfers between devices, shifted(): return lax.ppermute(block, axis, route)  25.2 us
    dot_general x5, matrix products, contribute(): return jnp.dot(kern, coef_rows, preferred_element_type=jnp.float32)  24 us
    all_to_all x1, starting transfers between devices, replace_panel_for(): lax.all_to_all(jnp.stack([my_tile for _ in range(lax.axis_size(ax_name))]...  7.21 us
  transfers between devices with their start and end apart: 9, of which 5 were waited for; matrix products, arithmetic and copies ran while one was open for 21% of the time, Pallas kernels for 0%

profile of v1, /device:TPU:2, one launch (start us, length us, event | category | flops | bytes accessed | tf_op | source)
XLA Modules:
  0.0 100.4 jit_solution(10416559102916016629)
XLA Ops:
  0.0 1.5 %stack.2 = bf16[16,64,128]{2,1,0:T(8,128)(2,1)} broadcast(bf16[64,128]{1,0:T(8,128)(2,1)} %param.5), dimensions={1,2} | broadcast | bytes 278528 | tf_op jit(solution)/shard_map/stack | solution.py:12
  1.6 7.2 %all-to-all-start = ((bf16[16,64,128]{2,1,0:T(8,128)(2,1)}), bf16[16,64,128]{2,1,0:T(8,128)(2,1)S(1)}, u32[]{:S(2)}, u32[]{:S(2)}) async-start(bf16[16,64,128]{2,1,0:T(8,128)(2,1)} %stack.2), calls=%async_computation | async-start | bytes 524288 | tf_op jit(solution)/shard_map/all_to_all | solution.py:11
  8.8 4.3 %collective-permute-start.3 = (bf16[1024,256]{1,0:T(8,128)(2,1)}, bf16[1024,256]{1,0:T(8,128)(2,1)S(1)}, u32[]{:S(2)}, u32[]{:S(2)}) collective-permute-start(bf16[1024,256]{1,0:T(8,128)(2,1)} %param.6), channel_id=1, source_target_pairs={{0,16},{16,32},{32,48},{48,64},{64,80},{80,96},{96,112},{112,128},... | collective-permute-start | bytes 1572872 | tf_op jit(solution)/shard_map/ppermute | solution.py:24
  13.1 6.1 %collective-permute-start.1 = (bf16[1024,256]{1,0:T(8,128)(2,1)}, bf16[1024,256]{1,0:T(8,128)(2,1)S(1)}, u32[]{:S(2)}, u32[]{:S(2)}) collective-permute-start(bf16[1024,256]{1,0:T(8,128)(2,1)} %param.6), channel_id=1, source_target_pairs={{0,32},{16,48},{32,64},{48,80},{64,96},{80,112},{96,128},{112,144}... | collective-permute-start | bytes 1572872 | tf_op jit(solution)/shard_map/ppermute | solution.py:24
  19.3 0.6 fusion.50
  23.0 1.2 %multiply_reduce_fusion.5 = f32[1024]{0:T(1024)S(1)} fusion(bf16[1024,128]{1,0:T(8,128)(2,1)} %param.4), kind=kLoop, calls=%fused_computation.35 | loop fusion | flops 392192 | bytes 266240 | tf_op jit(solution)/shard_map/reduce_sum | solution.py:29
  24.2 6.6 %collective-permute-start.6 = (bf16[1024,128]{1,0:T(8,128)(2,1)S(1)}, bf16[1024,128]{1,0:T(8,128)(2,1)S(1)}, u32[]{:S(2)}, u32[]{:S(2)}) collective-permute-start(bf16[1024,128]{1,0:T(8,128)(2,1)S(1)} %bitcast.21), channel_id=1, source_target_pairs={{32,0},{48,16},{64,32},{80,48},{96,64},{112,80},{128,96},{144,112}... | collective-permute-start | bytes 786440 | tf_op jit(solution)/shard_map/ppermute | solution.py:24
  30.9 2.6 %collective-permute-start.4 = (bf16[1024,128]{1,0:T(8,128)(2,1)S(1)}, bf16[1024,128]{1,0:T(8,128)(2,1)S(1)}, u32[]{:S(2)}, u32[]{:S(2)}) collective-permute-start(bf16[1024,128]{1,0:T(8,128)(2,1)S(1)} %bitcast.22), channel_id=1, source_target_pairs={{16,0},{32,16},{48,32},{64,48},{80,64},{96,80},{112,96},{128,112},... | collective-permute-start | bytes 786440 | tf_op jit(solution)/shard_map/ppermute | solution.py:24
  33.4 3.3 %collective-permute-start.2 = (bf16[1024,128]{1,0:T(8,128)(2,1)S(1)}, bf16[1024,128]{1,0:T(8,128)(2,1)S(1)}, u32[]{:S(2)}, u32[]{:S(2)}) collective-permute-start(bf16[1024,128]{1,0:T(8,128)(2,1)S(1)} %bitcast.23), channel_id=1, source_target_pairs={{0,16},{16,32},{32,48},{48,64},{64,80},{80,96},{96,112},{112,128},... | collective-permute-start | bytes 786440 | tf_op jit(solution)/shard_map/ppermute | solution.py:24
  36.7 0.2 multiply_reduce_fusion.4
  37.0 4.0 %fusion.19 = f32[1024,256]{1,0:T(8,128)} fusion(bf16[1024,256]{1,0:T(8,128)(2,1)S(1)} %copy-done.2, bf16[1024,128]{1,0:T(8,128)(2,1)S(1)} %copy-done.1, bf16[1024,128]{1,0:T(8,128)(2,1)S(1)} %bitcast.24, f32[]{:T(128)} %bitcast.1, f32[1024]{0:T(1024)S(1)} %add.91, f32[1024]{0:T(1024)S(1)} %multiply_reduce_fusion.5), kind=kOutput, calls=%fused_computation.24 | convolution fusion | flops 819986432 | bytes 2105348 | tf_op jit(solution)/shard_map/dot_general | solution.py:46
  41.1 2.3 %collective-permute-done.6 = bf16[1024,128]{1,0:T(8,128)(2,1)S(1)} collective-permute-done((bf16[1024,128]{1,0:T(8,128)(2,1)S(1)}, bf16[1024,128]{1,0:T(8,128)(2,1)S(1)}, u32[]{:S(2)}, u32[]{:S(2)}) %collective-permute-start.6) | collective-permute-done | bytes 262176 | tf_op jit(solution)/shard_map/ppermute | solution.py:24
  43.4 5.7 %collective-permute-start = (bf16[1024,128]{1,0:T(8,128)(2,1)S(1)}, bf16[1024,128]{1,0:T(8,128)(2,1)S(1)}, u32[]{:S(2)}, u32[]{:S(2)}) collective-permute-start(bf16[1024,128]{1,0:T(8,128)(2,1)S(1)} %bitcast.25), channel_id=1, source_target_pairs={{0,32},{16,48},{32,64},{48,80},{64,96},{80,112},{96,128},{112,144}... | collective-permute-start | bytes 786440 | tf_op jit(solution)/shard_map/ppermute | solution.py:24
  49.1 0.2 multiply_reduce_fusion
  49.5 3.2 %collective-permute-start.7 = (bf16[1024,256]{1,0:T(8,128)(2,1)S(1)}, bf16[1024,256]{1,0:T(8,128)(2,1)}, u32[]{:S(2)}, u32[]{:S(2)}) collective-permute-start(bf16[1024,256]{1,0:T(8,128)(2,1)S(1)} %copy-done.2), channel_id=1, source_target_pairs={{32,0},{48,16},{64,32},{80,48},{96,64},{112,80},{128,96},{144,112}... | collective-permute-start | bytes 1572872 | tf_op jit(solution)/shard_map/ppermute | solution.py:24
  52.7 0.2 multiply_reduce_fusion.1
  52.9 7.9 %collective-permute-done.2 = bf16[1024,128]{1,0:T(8,128)(2,1)S(1)} collective-permute-done((bf16[1024,128]{1,0:T(8,128)(2,1)S(1)}, bf16[1024,128]{1,0:T(8,128)(2,1)S(1)}, u32[]{:S(2)}, u32[]{:S(2)}) %collective-permute-start.2) | collective-permute-done | bytes 262176 | tf_op jit(solution)/shard_map/ppermute | solution.py:24
  60.8 4.3 %collective-permute-start.5 = (bf16[1024,256]{1,0:T(8,128)(2,1)S(1)}, bf16[1024,256]{1,0:T(8,128)(2,1)}, u32[]{:S(2)}, u32[]{:S(2)}) collective-permute-start(bf16[1024,256]{1,0:T(8,128)(2,1)S(1)} %copy-done.2), channel_id=1, source_target_pairs={{16,0},{32,16},{48,32},{64,48},{80,64},{96,80},{112,96},{128,112},... | collective-permute-start | bytes 1572872 | tf_op jit(solution)/shard_map/ppermute | solution.py:24
  65.4 7.6 %collective-permute-done = bf16[1024,128]{1,0:T(8,128)(2,1)S(1)} collective-permute-done((bf16[1024,128]{1,0:T(8,128)(2,1)S(1)}, bf16[1024,128]{1,0:T(8,128)(2,1)S(1)}, u32[]{:S(2)}, u32[]{:S(2)}) %collective-permute-start) | collective-permute-done | bytes 262176 | tf_op jit(solution)/shard_map/ppermute | solution.py:24
  73.2 4.1 %fusion.17 = f32[1024,256]{1,0:T(8,128)} fusion(bf16[1024,256]{1,0:T(8,128)(2,1)S(1)} %collective-permute-done.3, bf16[1024,128]{1,0:T(8,128)(2,1)S(1)} %copy-done.1, bf16[1024,128]{1,0:T(8,128)(2,1)S(1)} %collective-permute-done.2, f32[]{:T(128)} %bitcast.3, f32[1024]{0:T(1024)S(1)} %multiply_reduce_fusion.2, f32[1024]{0:T(1024)S(1)} %multiply_reduce_fusion.5), kind=kOutput, calls=%fused_computation.22 | convolution fusion | flops 819986432 | bytes 2105348 | tf_op jit(solution)/shard_map/dot_general | solution.py:46
  77.3 5.1 %fusion.15 = f32[1024,256]{1,0:T(8,128)} fusion(bf16[1024,256]{1,0:T(8,128)(2,1)} %collective-permute-done.7, bf16[1024,128]{1,0:T(8,128)(2,1)S(1)} %copy-done.1, bf16[1024,128]{1,0:T(8,128)(2,1)S(1)} %collective-permute-done.6, f32[]{:T(128)} %bitcast.5, f32[1024]{0:T(1024)S(1)} %multiply_reduce_fusion, f32[1024]{0:T(1024)S(1)} %multiply_reduce_fusion.5), kind=kOutput, calls=%fused_computation.20 | convolution fusion | flops 819986432 | bytes 2105348 | tf_op jit(solution)/shard_map/dot_general | solution.py:46
  82.4 7.2 %collective-permute-done.5 = bf16[1024,256]{1,0:T(8,128)(2,1)} collective-permute-done((bf16[1024,256]{1,0:T(8,128)(2,1)S(1)}, bf16[1024,256]{1,0:T(8,128)(2,1)}, u32[]{:S(2)}, u32[]{:S(2)}) %collective-permute-start.5) | collective-permute-done | bytes 524320 | tf_op jit(solution)/shard_map/ppermute | solution.py:24
  89.7 5.1 %fusion.16 = f32[1024,256]{1,0:T(8,128)} fusion(bf16[1024,256]{1,0:T(8,128)(2,1)} %collective-permute-done.5, bf16[1024,128]{1,0:T(8,128)(2,1)S(1)} %copy-done.1, bf16[1024,128]{1,0:T(8,128)(2,1)S(1)} %collective-permute-done.4, f32[]{:T(128)} %bitcast.4, f32[1024]{0:T(1024)S(1)} %multiply_reduce_fusion.1, f32[1024]{0:T(1024)S(1)} %multiply_reduce_fusion.5), kind=kOutput, calls=%fused_computation.21 | convolution fusion | flops 819986432 | bytes 2105348 | tf_op jit(solution)/shard_map/dot_general | solution.py:46
  94.8 5.6 %fusion.24 = bf16[1024,256]{1,0:T(8,128)(2,1)} fusion(f32[1024,256]{1,0:T(8,128)} %fusion.15, f32[1024,256]{1,0:T(8,128)} %fusion.16, f32[1024,256]{1,0:T(8,128)} %fusion.17, f32[1024,256]{1,0:T(8,128)} %fusion.19, bf16[1024,256]{1,0:T(8,128)(2,1)S(1)} %collective-permute-done.1, bf16[1024,128]{1,0:T(8,128)(2,1)S(1)} %copy-done.1, ...), kind=kOutput, calls=%fused_computation.29 | convolution fusion | flops 821297152 | bytes 5775364 | tf_op jit(solution)/shard_map/dot_general | solution.py:46
  (15 shorter events, 0.7 us)
Async XLA Ops:
  0.0 19.2 %copy-start = (s32[32,5]{0,1:T(8,128)S(1)}, s32[32,5]{0,1:T(8,128)}, u32[]{:S(2)}) copy-start(s32[32,5]{0,1:T(8,128)} %param.7) | copy-start | bytes 1924
  0.0 37.0 %copy-start.2 = (bf16[1024,256]{1,0:T(8,128)(2,1)S(1)}, bf16[1024,256]{1,0:T(8,128)(2,1)}, u32[]{:S(2)}) copy-start(bf16[1024,256]{1,0:T(8,128)(2,1)} %param.6) | copy-start | bytes 1572868
  0.0 37.0 %copy-start.1 = (bf16[1024,128]{1,0:T(8,128)(2,1)S(1)}, bf16[1024,128]{1,0:T(8,128)(2,1)}, u32[]{:S(2)}) copy-start(bf16[1024,128]{1,0:T(8,128)(2,1)} %param.4) | copy-start | bytes 786436
  1.6 22.7 %all-to-all-start = ((bf16[16,64,128]{2,1,0:T(8,128)(2,1)}), bf16[16,64,128]{2,1,0:T(8,128)(2,1)S(1)}, u32[]{:S(2)}, u32[]{:S(2)}) async-start(bf16[16,64,128]{2,1,0:T(8,128)(2,1)} %stack.2), calls=%async_computation | async-start | bytes 524288 | tf_op jit(solution)/shard_map/all_to_all | solution.py:11
  8.8 64.4 %collective-permute-start.3 = (bf16[1024,256]{1,0:T(8,128)(2,1)}, bf16[1024,256]{1,0:T(8,128)(2,1)S(1)}, u32[]{:S(2)}, u32[]{:S(2)}) collective-permute-start(bf16[1024,256]{1,0:T(8,128)(2,1)} %param.6), channel_id=1, source_target_pairs={{0,16},{16,32},{32,48},{48,64},{64,80},{80,96},{96,112},{112,128},... | collective-permute-start | bytes 1572872 | tf_op jit(solution)/shard_map/ppermute | solution.py:24
  13.1 81.7 %collective-permute-start.1 = (bf16[1024,256]{1,0:T(8,128)(2,1)}, bf16[1024,256]{1,0:T(8,128)(2,1)S(1)}, u32[]{:S(2)}, u32[]{:S(2)}) collective-permute-start(bf16[1024,256]{1,0:T(8,128)(2,1)} %param.6), channel_id=1, source_target_pairs={{0,32},{16,48},{32,64},{48,80},{64,96},{80,112},{96,128},{112,144}... | collective-permute-start | bytes 1572872 | tf_op jit(solution)/shard_map/ppermute | solution.py:24
  24.2 19.2 %collective-permute-start.6 = (bf16[1024,128]{1,0:T(8,128)(2,1)S(1)}, bf16[1024,128]{1,0:T(8,128)(2,1)S(1)}, u32[]{:S(2)}, u32[]{:S(2)}) collective-permute-start(bf16[1024,128]{1,0:T(8,128)(2,1)S(1)} %bitcast.21), channel_id=1, source_target_pairs={{32,0},{48,16},{64,32},{80,48},{96,64},{112,80},{128,96},{144,112}... | collective-permute-start | bytes 786440 | tf_op jit(solution)/shard_map/ppermute | solution.py:24
  30.9 18.6 %collective-permute-start.4 = (bf16[1024,128]{1,0:T(8,128)(2,1)S(1)}, bf16[1024,128]{1,0:T(8,128)(2,1)S(1)}, u32[]{:S(2)}, u32[]{:S(2)}) collective-permute-start(bf16[1024,128]{1,0:T(8,128)(2,1)S(1)} %bitcast.22), channel_id=1, source_target_pairs={{16,0},{32,16},{48,32},{64,48},{80,64},{96,80},{112,96},{128,112},... | collective-permute-start | bytes 786440 | tf_op jit(solution)/shard_map/ppermute | solution.py:24
  33.4 27.4 %collective-permute-start.2 = (bf16[1024,128]{1,0:T(8,128)(2,1)S(1)}, bf16[1024,128]{1,0:T(8,128)(2,1)S(1)}, u32[]{:S(2)}, u32[]{:S(2)}) collective-permute-start(bf16[1024,128]{1,0:T(8,128)(2,1)S(1)} %bitcast.23), channel_id=1, source_target_pairs={{0,16},{16,32},{32,48},{48,64},{64,80},{80,96},{96,112},{112,128},... | collective-permute-start | bytes 786440 | tf_op jit(solution)/shard_map/ppermute | solution.py:24
  43.4 29.6 %collective-permute-start = (bf16[1024,128]{1,0:T(8,128)(2,1)S(1)}, bf16[1024,128]{1,0:T(8,128)(2,1)S(1)}, u32[]{:S(2)}, u32[]{:S(2)}) collective-permute-start(bf16[1024,128]{1,0:T(8,128)(2,1)S(1)} %bitcast.25), channel_id=1, source_target_pairs={{0,32},{16,48},{32,64},{48,80},{64,96},{80,112},{96,128},{112,144}... | collective-permute-start | bytes 786440 | tf_op jit(solution)/shard_map/ppermute | solution.py:24
  49.5 27.9 %collective-permute-start.7 = (bf16[1024,256]{1,0:T(8,128)(2,1)S(1)}, bf16[1024,256]{1,0:T(8,128)(2,1)}, u32[]{:S(2)}, u32[]{:S(2)}) collective-permute-start(bf16[1024,256]{1,0:T(8,128)(2,1)S(1)} %copy-done.2), channel_id=1, source_target_pairs={{32,0},{48,16},{64,32},{80,48},{96,64},{112,80},{128,96},{144,112}... | collective-permute-start | bytes 1572872 | tf_op jit(solution)/shard_map/ppermute | solution.py:24
  60.8 28.9 %collective-permute-start.5 = (bf16[1024,256]{1,0:T(8,128)(2,1)S(1)}, bf16[1024,256]{1,0:T(8,128)(2,1)}, u32[]{:S(2)}, u32[]{:S(2)}) collective-permute-start(bf16[1024,256]{1,0:T(8,128)(2,1)S(1)} %copy-done.2), channel_id=1, source_target_pairs={{16,0},{32,16},{48,32},{64,48},{80,64},{96,80},{112,96},{128,112},... | collective-permute-start | bytes 1572872 | tf_op jit(solution)/shard_map/ppermute | solution.py:24
